TPU v7x, 256 devices: a whole 4x4x8 slice. The times are simulated.
256 devices in a mesh: cell: 32 (over z, y_hi, core), period: 8 (over x, y_lo).
Axes of the slice: x: 4, y: 4 (y_hi: 2, y_lo: 2; y = y_hi * 2 + y_lo), z: 8, core: 2. Of those that a mesh axis runs over, the one named last changes fastest.
Arguments:
- footprints: float32 [32, 16, 32768], P(None, 'period', 'cell'), may hold values from -16 to 16
- cell_coords: int32 [2, 32768], P(None, 'cell'), may hold values from 0 to 255, as said below
- obs_period: int32 [32], replicated, may hold values from 0 to 15
- temporal_cov: float32 [16, 16], replicated, may hold values from -1.5 to 1.5
Outputs:
- hq_field: float32 [32, 16, 32768], P(None, 'period', 'cell')
- hqh_gram: float32 [32, 32], replicated
Inputs may be any that keep to these rules, and one draw needn't show every extreme that they name: `cell_coords`: cells sit at distinct grid points that together fill the rectangle of first coordinates 0 to 255 and second coordinates 0 to 127.
All inputs are finite; a program needn't handle non-finite values.
Results may differ from a plain program's by a relative error of at most 0.0003.
Values sent between devices are 32-bit elements; how exact they have to be, the bound alone decides.
No kernel may reach another device: no remote copies, remote signals or barrier semaphores. Data moves between devices by JAX's collectives and lax.ppermute only.
A program may use at most 64 MiB of HBM per device.

v0:
```python
import jax
import jax.numpy as jnp
from jax import lax
from jax.sharding import PartitionSpec as P

LENGTH_SCALE = 48.0
BLOCK_LIMIT = 4096


def covariance_tile(first_xy, second_xy):
    delta_x = first_xy[0][:, None] - second_xy[0][None, :]
    delta_y = first_xy[1][:, None] - second_xy[1][None, :]
    return jnp.exp(-jnp.sqrt(delta_x * delta_x + delta_y * delta_y) / LENGTH_SCALE)


def block_size(total_width, unit_width):
    unit_count = total_width // unit_width
    best_count = 1
    for factor in range(1, unit_count + 1):
        if unit_count % factor == 0 and factor * unit_width <= max(BLOCK_LIMIT, unit_width):
            best_count = factor
    return best_count * unit_width


def on_device(footprints, cell_coords, obs_period, temporal_cov):
    obs_count, per_local, cell_local = footprints.shape
    flat_count = obs_count * per_local
    period_first = lax.axis_index("period") * per_local
    period_ids = period_first + jnp.arange(per_local, dtype=jnp.int32)
    keep = (period_ids[None, :, None] <= obs_period[:, None, None]).astype(jnp.float32)
    masked = footprints * keep
    flat_rows = masked.reshape(flat_count, cell_local)
    local_places = cell_coords.astype(jnp.float32)
    empty = jnp.zeros((flat_count, cell_local), jnp.float32)
    piece_rows = lax.all_gather(flat_rows, "cell", axis=1, tiled=True)
    piece_places = lax.all_gather(local_places, "cell", axis=1, tiled=True)
    piece_width = piece_rows.shape[1]
    block_width = block_size(piece_width, cell_local)

    def add_block(block_index, running_sum):
        offset = block_index * block_width
        part_rows = lax.dynamic_slice_in_dim(piece_rows, offset, block_width, 1)
        part_places = lax.dynamic_slice_in_dim(piece_places, offset, block_width, 1)
        tile = covariance_tile(part_places, local_places)
        return running_sum + jnp.dot(
            part_rows, tile, precision=lax.Precision.HIGHEST, preferred_element_type=jnp.float32
        )

    spatial_flat = lax.fori_loop(0, piece_width // block_width, add_block, empty)
    spatial = spatial_flat.reshape(obs_count, per_local, cell_local)
    piece = lax.all_gather(spatial, "period", axis=1, tiled=True)
    weights = lax.dynamic_slice(temporal_cov, (period_first, 0), (per_local, piece.shape[1]))
    hq_field = jnp.einsum("tu,nuj->ntj", weights, piece, precision=lax.Precision.HIGHEST)
    partial_gram = jnp.einsum("ntj,mtj->nm", hq_field, masked, precision=lax.Precision.HIGHEST)
    hqh_gram = lax.psum(partial_gram, ("cell", "period"))
    return (hq_field, hqh_gram)


def solution(mesh):
    return jax.shard_map(
        on_device,
        mesh=mesh,
        in_specs=(P(None, "period", "cell"), P(None, "cell"), P(), P()),
        out_specs=(P(None, "period", "cell"), P()),
        check_vma=False,
    )
```

profile of v0, /device:TPU:1, one launch (start us, length us, event | category | flops | bytes accessed | tf_op | source)
XLA Modules:
  0.0 412.7 jit_solution(13719887616135554057)
XLA Ops:
  7.2 0.0 copy-start
  7.2 0.0 all-gather.3.cloned.1.call-start
  7.2 0.7 compare_convert_fusion
  8.0 0.1 copy.15
  8.1 1.1 broadcast_multiply_fusion
  9.2 0.9 reshape.51
  10.0 0.0 all-gather.3.cloned.1.call-update
  10.1 0.0 all-gather.5.cloned.1.call-start
  10.1 0.7 convert_element_type.12
  10.8 47.3 %all_gather.10 = f32[2,32768]{1,0:T(2,128)S(1)} all-gather(f32[2,1024]{1,0:T(2,128)S(1)} %convert_element_type.12), channel_id=1, replica_groups=mesh['cell'=32,'period'=8] {'cell'}, dimensions={1}, use_global_device_ids=true | all-gather | bytes 270336 | tf_op jit(solution)/shard_map/all_gather | solution.py:36
  58.1 58.6 %all-gather.3.cloned.1.call-done = f32[64,32768]{1,0:T(8,128)} async-done(((f32[64,1024]{1,0:T(8,128)}), f32[64,32768]{1,0:T(8,128)}) %all-gather.3.cloned.1.call-update) | async-done | bytes 8388624 | tf_op jit(solution)/shard_map/all_gather | solution.py:35
  116.7 157.3 %while.14 = (s32[]{:T(128)}, f32[64,1024]{1,0:T(8,128)S(1)}, f32[64,32768]{1,0:T(8,128)}, f32[2,32768]{1,0:T(2,128)S(1)}, f32[2,1024]{1,0:T(2,128)S(1)}, /*index...) while((s32[]{:T(128)}, f32[64,1024]{1,0:T(8,128)S(1)}, f32[64,32768]{1,0:T(8,128)}, ...), condition=%wide.region_1.0_spmd.clone, body=%wide.region_0.0_spmd.clone.sunk | while | flops 3250716672 | bytes 1695933 | solution.py:49
  116.7 0.1 constant_dynamic-slice_fusion.2
  116.8 19.5 %fusion.39 = f32[64,1024]{1,0:T(8,128)S(1)} fusion(f32[1024]{0:T(1024)S(1)} %bitcast.22, f32[4096]{0:T(1024)S(1)} %bitcast.20, f32[1024]{0:T(1024)S(1)} %bitcast.21, f32[4096]{0:T(1024)S(1)} %bitcast.19, f32[64,32768]{1,0:T(8,128)} %get-tuple-element.190, s32[]{:T(128)S(6)} %select_n.14, f32[64,1024]{1,0:T(8,128)S(1)} %get-tuple-element.179, ...), kind=kOutput, calls=%fused_computation.15.clone.1 | convolution fusion | flops 3250716672 | bytes 1613829 | tf_op jit(solution)/shard_map/while/body/eval_jaxpr/dot_general | solution.py:45
  136.3 0.1 constant_dynamic-slice_fusion.2
  136.4 19.5 %fusion.39 = f32[64,1024]{1,0:T(8,128)S(1)} fusion(f32[1024]{0:T(1024)S(1)} %bitcast.22, f32[4096]{0:T(1024)S(1)} %bitcast.20, f32[1024]{0:T(1024)S(1)} %bitcast.21, f32[4096]{0:T(1024)S(1)} %bitcast.19, f32[64,32768]{1,0:T(8,128)} %get-tuple-element.190, s32[]{:T(128)S(6)} %select_n.14, f32[64,1024]{1,0:T(8,128)S(1)} %get-tuple-element.179, ...), kind=kOutput, calls=%fused_computation.15.clone.1 | convolution fusion | flops 3250716672 | bytes 1613829 | tf_op jit(solution)/shard_map/while/body/eval_jaxpr/dot_general | solution.py:45
  156.0 0.1 constant_dynamic-slice_fusion.2
  156.1 19.5 %fusion.39 = f32[64,1024]{1,0:T(8,128)S(1)} fusion(f32[1024]{0:T(1024)S(1)} %bitcast.22, f32[4096]{0:T(1024)S(1)} %bitcast.20, f32[1024]{0:T(1024)S(1)} %bitcast.21, f32[4096]{0:T(1024)S(1)} %bitcast.19, f32[64,32768]{1,0:T(8,128)} %get-tuple-element.190, s32[]{:T(128)S(6)} %select_n.14, f32[64,1024]{1,0:T(8,128)S(1)} %get-tuple-element.179, ...), kind=kOutput, calls=%fused_computation.15.clone.1 | convolution fusion | flops 3250716672 | bytes 1613829 | tf_op jit(solution)/shard_map/while/body/eval_jaxpr/dot_general | solution.py:45
  175.6 0.1 constant_dynamic-slice_fusion.2
  175.7 19.5 %fusion.39 = f32[64,1024]{1,0:T(8,128)S(1)} fusion(f32[1024]{0:T(1024)S(1)} %bitcast.22, f32[4096]{0:T(1024)S(1)} %bitcast.20, f32[1024]{0:T(1024)S(1)} %bitcast.21, f32[4096]{0:T(1024)S(1)} %bitcast.19, f32[64,32768]{1,0:T(8,128)} %get-tuple-element.190, s32[]{:T(128)S(6)} %select_n.14, f32[64,1024]{1,0:T(8,128)S(1)} %get-tuple-element.179, ...), kind=kOutput, calls=%fused_computation.15.clone.1 | convolution fusion | flops 3250716672 | bytes 1613829 | tf_op jit(solution)/shard_map/while/body/eval_jaxpr/dot_general | solution.py:45
  195.3 0.1 constant_dynamic-slice_fusion.2
  195.4 19.5 %fusion.39 = f32[64,1024]{1,0:T(8,128)S(1)} fusion(f32[1024]{0:T(1024)S(1)} %bitcast.22, f32[4096]{0:T(1024)S(1)} %bitcast.20, f32[1024]{0:T(1024)S(1)} %bitcast.21, f32[4096]{0:T(1024)S(1)} %bitcast.19, f32[64,32768]{1,0:T(8,128)} %get-tuple-element.190, s32[]{:T(128)S(6)} %select_n.14, f32[64,1024]{1,0:T(8,128)S(1)} %get-tuple-element.179, ...), kind=kOutput, calls=%fused_computation.15.clone.1 | convolution fusion | flops 3250716672 | bytes 1613829 | tf_op jit(solution)/shard_map/while/body/eval_jaxpr/dot_general | solution.py:45
  214.9 0.1 constant_dynamic-slice_fusion.2
  215.0 19.5 %fusion.39 = f32[64,1024]{1,0:T(8,128)S(1)} fusion(f32[1024]{0:T(1024)S(1)} %bitcast.22, f32[4096]{0:T(1024)S(1)} %bitcast.20, f32[1024]{0:T(1024)S(1)} %bitcast.21, f32[4096]{0:T(1024)S(1)} %bitcast.19, f32[64,32768]{1,0:T(8,128)} %get-tuple-element.190, s32[]{:T(128)S(6)} %select_n.14, f32[64,1024]{1,0:T(8,128)S(1)} %get-tuple-element.179, ...), kind=kOutput, calls=%fused_computation.15.clone.1 | convolution fusion | flops 3250716672 | bytes 1613829 | tf_op jit(solution)/shard_map/while/body/eval_jaxpr/dot_general | solution.py:45
  234.6 0.1 constant_dynamic-slice_fusion.2
  234.7 19.5 %fusion.39 = f32[64,1024]{1,0:T(8,128)S(1)} fusion(f32[1024]{0:T(1024)S(1)} %bitcast.22, f32[4096]{0:T(1024)S(1)} %bitcast.20, f32[1024]{0:T(1024)S(1)} %bitcast.21, f32[4096]{0:T(1024)S(1)} %bitcast.19, f32[64,32768]{1,0:T(8,128)} %get-tuple-element.190, s32[]{:T(128)S(6)} %select_n.14, f32[64,1024]{1,0:T(8,128)S(1)} %get-tuple-element.179, ...), kind=kOutput, calls=%fused_computation.15.clone.1 | convolution fusion | flops 3250716672 | bytes 1613829 | tf_op jit(solution)/shard_map/while/body/eval_jaxpr/dot_general | solution.py:45
  254.2 0.1 constant_dynamic-slice_fusion.2
  254.3 19.5 %fusion.39 = f32[64,1024]{1,0:T(8,128)S(1)} fusion(f32[1024]{0:T(1024)S(1)} %bitcast.22, f32[4096]{0:T(1024)S(1)} %bitcast.20, f32[1024]{0:T(1024)S(1)} %bitcast.21, f32[4096]{0:T(1024)S(1)} %bitcast.19, f32[64,32768]{1,0:T(8,128)} %get-tuple-element.190, s32[]{:T(128)S(6)} %select_n.14, f32[64,1024]{1,0:T(8,128)S(1)} %get-tuple-element.179, ...), kind=kOutput, calls=%fused_computation.15.clone.1 | convolution fusion | flops 3250716672 | bytes 1613829 | tf_op jit(solution)/shard_map/while/body/eval_jaxpr/dot_general | solution.py:45
  274.0 0.1 reshape.52
  274.2 0.8 copy.16
  275.0 0.0 all-gather.5.cloned.1.call-update
  275.0 48.4 %all-gather.5.cloned.1.call-done = f32[32,16,1024]{2,0,1:T(8,128)} async-done(((f32[32,2,1024]{2,0,1:T(8,128)}), f32[32,16,1024]{2,0,1:T(8,128)}) %all-gather.5.cloned.1.call-update) | async-done | bytes 2097168 | tf_op jit(solution)/shard_map/all_gather | solution.py:51
  323.4 0.0 copy-done
  323.4 3.9 fusion.23
  327.3 0.0 copy-start.1
  327.3 0.5 convolution_bitcast_fusion
  327.7 78.1 %psum.7 = f32[32,32]{1,0:T(8,128)} all-reduce(f32[32,32]{1,0:T(8,128)S(1)} %convolution_bitcast_fusion), channel_id=1, replica_groups=mesh['cell'=32,'period'=8] {'cell','period'}, use_global_device_ids=true, to_apply=%region_2.0 | all-reduce | flops 1024 | bytes 8192 | tf_op jit(solution)/shard_map/psum | solution.py:55
  405.8 0.0 copy-done.1
  (10 shorter events, 0.1 us)
Async XLA Ops:
  7.2 316.2 %copy-start = (f32[16,16]{1,0:T(8,128)S(1)}, f32[16,16]{1,0:T(8,128)}, u32[]{:S(2)}) copy-start(f32[16,16]{1,0:T(8,128)} %param.9) | copy-start | bytes 3076
  7.2 109.5 %all-gather.3.cloned.1.call-start = ((), (), s32[]{:S(2)}) async-start(), calls=%async_computation | async-start | bytes 8650752 | tf_op jit(solution)/shard_map/all_gather | solution.py:35
  10.1 313.3 %all-gather.5.cloned.1.call-start = ((), (), s32[]{:S(2)}) async-start(), calls=%async_computation.1 | async-start | bytes 2359296 | tf_op jit(solution)/shard_map/all_gather | solution.py:51
  327.3 78.6 %copy-start.1 = (f32[32,2,1024]{2,1,0:T(2,128)}, f32[32,2,1024]{2,1,0:T(2,128)S(1)}, u32[]{:S(2)}) copy-start(f32[32,2,1024]{2,1,0:T(2,128)S(1)} %fusion.23) | copy-start | bytes 786436
Sparse Core Ops, SparseCore 0:
  11.4 105.2 all-gather.2
  275.1 48.2 all-gather.4
where the time goes:
time: 413 us
  matrix products  160 us (39%)
  blocking collectives  125 us (30%)
  waiting for transfers between devices  107 us (26%)
  between operations  14.1 us (3%)
    dot_general x8, matrix products, add_block(): jnp.dot(part_rows, tile, precision=lax.Precision.HIGHEST, preferred_eleme...  156 us
    psum x1, blocking collectives, on_device(): hqh_gram = lax.psum(partial_gram, ('cell', 'period'))  78.1 us
    all_gather x1, waiting for transfers between devices, on_device(): piece_rows = lax.all_gather(flat_rows, 'cell', axis=1, tiled=True)  58.6 us
    all_gather x1, waiting for transfers between devices, on_device(): piece = lax.all_gather(spatial, 'period', axis=1, tiled=True)  48.4 us
    all_gather x1, blocking collectives, on_device(): piece_places = lax.all_gather(local_places, 'cell', axis=1, tiled=True)  47.3 us
  transfers between devices with their start and end apart: 2, of which 2 were waited for; matrix products, arithmetic and copies ran while one was open for 0% of the time, Pallas kernels for 0%

commit v1 on v0

v1 whole, which is shorter than its diff:
```python
import jax
import jax.numpy as jnp
import numpy as np
from jax import lax
from jax.experimental import pallas as pl
from jax.experimental.pallas import tpu as pltpu
from jax.sharding import Mesh, PartitionSpec as P
LENGTH_SCALE=48.0
W,H=256,128
def real_basis(n, keep):
    pos=np.arange(keep)[None,:]; rows=[]
    k=np.arange(n)[:,None]
    freq=np.where(k<=n//2,k,n-k)
    ang=2*np.pi*((freq*pos)%n)/n
    b=np.where(k<=n//2,np.cos(ang),np.sin(ang))*np.sqrt(2.0/n)
    b[0]/=np.sqrt(2.0); b[n//2]/=np.sqrt(2.0)
    return b, np.where(np.arange(n)<=n//2,np.arange(n),n-np.arange(n))
def constants():
    bx,fx=real_basis(2*W,W); by,fy=real_basis(2*H,H)
    dx=np.minimum(np.arange(2*W),2*W-np.arange(2*W)); dy=np.minimum(np.arange(2*H),2*H-np.arange(2*H))
    cov=np.exp(-np.sqrt(dy[:,None]**2.0+dx[None,:]**2.0)/LENGTH_SCALE)
    lam=np.real(np.fft.fft2(cov))
    lam=lam[fy][:,fx]
    return bx,by,lam
HI=lax.Precision.HIGHEST
NT=(((1,),(1,)),((),()))
def spatial_kernel(inp_ref,bxt_ref,bxi_ref,by_ref,byt_ref,lam_ref,out_ref,acc_ref,tab_ref):
    n_lists=inp_ref.shape[0]; L=inp_ref.shape[2]
    acc_ref[...]=jnp.zeros_like(acc_ref)
    def onehot(col,count):
        ids=lax.broadcasted_iota(jnp.int32,(count,L),0).astype(jnp.float32).astype(jnp.bfloat16)
        return ids==col.astype(jnp.bfloat16)
    def place(c,_):
        blk=inp_ref[c]
        xs=blk[2:3,:]; ys=blk[3:4,:]
        my=onehot(ys,H); mx=onehot(xs,W)
        parts=[]
        for r in range(2):
            f=blk[r:r+1,:]
            hi=f.astype(jnp.bfloat16); lo=(f-hi.astype(jnp.float32)).astype(jnp.bfloat16)
            lo2=(f-hi.astype(jnp.float32)-lo.astype(jnp.float32)).astype(jnp.bfloat16)
            for p in (hi,lo,lo2):
                parts.append(jnp.where(my,p,jnp.bfloat16(0)))
        a=jnp.concatenate(parts,0)
        b=jnp.where(mx,jnp.bfloat16(1),jnp.bfloat16(0))
        acc_ref[...]+=lax.dot_general(a,b,NT,preferred_element_type=jnp.float32)
        return 0
    lax.fori_loop(0,n_lists,place,0,unroll=4)
    for r in range(2):
        g=acc_ref[384*r:384*r+128,:]+(acc_ref[384*r+128:384*r+256,:]+acc_ref[384*r+256:384*r+384,:])
        u=jnp.dot(g,bxt_ref[...],precision=HI,preferred_element_type=jnp.float32)
        z=jnp.dot(by_ref[...],u,precision=HI,preferred_element_type=jnp.float32)
        z=z*lam_ref[...]
        v=jnp.dot(byt_ref[...],z,precision=HI,preferred_element_type=jnp.float32)
        ht=lax.dot_general(bxi_ref[...],v,NT,precision=HI,preferred_element_type=jnp.float32)
        hi=ht.astype(jnp.bfloat16); lo=(ht-hi.astype(jnp.float32)).astype(jnp.bfloat16)
        for xm in range(4):
            tab_ref[64*r:64*r+64,128*xm:128*xm+128]=hi[64*xm:64*xm+64,:]
            tab_ref[64*r:64*r+64,512+128*xm:512+128*xm+128]=lo[64*xm:64*xm+64,:]
    def pick(c,_):
        blk=inp_ref[c]
        xs=blk[2:3,:]; ys=blk[3:4,:]
        xm=jnp.floor(xs*(1.0/64)); xq=xs-64*xm
        my=onehot(ys,H)
        xmb=xm.astype(jnp.bfloat16)
        one=jnp.where(my,jnp.bfloat16(1),jnp.bfloat16(0))
        oh=jnp.concatenate([one*jnp.where(xmb==m,jnp.bfloat16(1),jnp.bfloat16(0)) for m in range(4)],0)
        t=jnp.dot(tab_ref[:,:512],oh,preferred_element_type=jnp.float32)+jnp.dot(tab_ref[:,512:],oh,preferred_element_type=jnp.float32)
        mq=lax.broadcasted_iota(jnp.int32,(64,L),0).astype(jnp.float32)==xq
        for r in range(2):
            o=jnp.sum(jnp.where(mq,t[64*r:64*r+64,:],0.0),0,keepdims=True)
            for s in range(L//128):
                out_ref[c,s,r:r+1,:]=o[:,128*s:128*s+128]
        return 0
    lax.fori_loop(0,n_lists,pick,0,unroll=4)
def spatial(inp,interpret=False):
    bx,by,lam=constants()
    f=lambda a: jnp.asarray(a.astype(np.float32))
    L=inp.shape[2]
    vm=pl.BlockSpec(memory_space=pltpu.VMEM)
    return pl.pallas_call(spatial_kernel,
        out_shape=jax.ShapeDtypeStruct((inp.shape[0],L//128,2,128),jnp.float32),
        in_specs=[vm]*6,out_specs=vm,
        scratch_shapes=[pltpu.VMEM((768,256),jnp.float32),pltpu.VMEM((128,1024),jnp.bfloat16)],
        interpret=interpret,
        name="spatial",
    )(inp,f(bx.T),f(bx.T),f(by),f(by.T),f(lam))


CELL = ("z", "y_hi", "core")
PERIOD = ("x", "y_lo")


def group_sum(values, axes, count):
    spread = jnp.broadcast_to(values[None], (count,) + values.shape)
    return jnp.sum(lax.all_to_all(spread, axes, 0, 0, tiled=True), axis=0)


def on_device(footprints, cell_coords, obs_period, temporal_cov):
    obs_count, per_local, cell_local = footprints.shape
    cell_size, period_size = 32, 8
    period_first = lax.axis_index(PERIOD) * per_local
    period_ids = period_first + jnp.arange(per_local, dtype=jnp.int32)
    keep = (period_ids[None, :, None] <= obs_period[:, None, None]).astype(jnp.float32)
    masked = footprints * keep
    places = jnp.broadcast_to(cell_coords.astype(jnp.float32)[None], (obs_count, 2, cell_local))
    rows = lax.all_to_all(jnp.concatenate([masked, places], 1), CELL, 0, 0, tiled=True)
    mixed_cells = spatial(rows)
    by_cell = lax.all_to_all(
        mixed_cells.reshape(cell_size * period_size, per_local, 128), CELL + PERIOD, 0, 0, tiled=True
    )
    by_cell = by_cell.reshape(obs_count, period_size * per_local, 128)
    mixed = jnp.einsum("tu,nuj->tnj", temporal_cov, by_cell, precision=lax.Precision.HIGHEST)
    mixed = lax.all_to_all(
        mixed.reshape(period_size, per_local, obs_count, 128), PERIOD, 0, 0, tiled=True
    )
    hq_field = jnp.transpose(mixed, (2, 1, 0, 3)).reshape(obs_count, per_local, cell_local)
    gram = jnp.einsum("ntj,mtj->nm", hq_field, masked, precision=lax.Precision.HIGHEST)
    gram = group_sum(gram.reshape(obs_count * obs_count), ("x", "y_lo", "core"), 16)
    gram = group_sum(gram, ("z", "y_hi"), 16)
    return (hq_field, gram.reshape(obs_count, obs_count))


def solution(mesh):
    fine = Mesh(mesh.devices.reshape(8, 2, 2, 4, 2), CELL + PERIOD)
    return jax.shard_map(
        on_device,
        mesh=fine,
        in_specs=(P(None, PERIOD, CELL), P(None, CELL), P(), P()),
        out_specs=(P(None, PERIOD, CELL), P()),
        check_vma=False,
    )
```

time: 413 us -> 124 us (0.30)
  matrix products: 160 us -> 0.75 us
  waiting for transfers between devices: 107 us -> 8.51 us
  blocking collectives: 125 us -> 73.3 us
  Pallas kernels: 0 us -> 31.3 us
  between operations: 14.1 us -> 0.74 us
    dot_general x9 -> x1, matrix products: 160 us -> 0.35 us  [on_device(): jnp.einsum('tu,nuj->tnj', temporal_cov, by_cell, precision=lax.Precision....]
    all_gather x2 -> x0, waiting for transfers between devices: 107 us -> none  [the longest x1 58.6 us: on_device(): piece_rows = lax.all_gather(flat_rows, 'cell', axis=1, tiled=True)]
    psum x1 -> x0, blocking collectives: 78.1 us -> none  [on_device(): hqh_gram = lax.psum(partial_gram, ('cell', 'period'))]
    all_to_all x0 -> x4, blocking collectives: none -> 73.3 us  [the longest x1 29.5 us: on_device(): lax.all_to_all(jnp.concatenate([masked, places], 1), CELL, 0, 0, tiled=True)]
    all_gather x1 -> x0, blocking collectives: 47.3 us -> none  [on_device(): piece_places = lax.all_gather(local_places, 'cell', axis=1, tiled=True)]
    pallas_call x0 -> x1, Pallas kernels: none -> 31.3 us  [spatial(): pl.pallas_call(spatial_kernel, out_shape=jax.ShapeDtypeStruct((inp.shape[...]
    all_to_all x0 -> x1, waiting for transfers between devices: none -> 8.51 us  [group_sum(): return jnp.sum(lax.all_to_all(spread, axes, 0, 0, tiled=True), axis=0)]
  transfers between devices with their start and end apart: 2 -> 1, of which waited for: 2 -> 1; matrix products, arithmetic and copies ran while one was open for 0% -> 1% of each run, Pallas kernels for 0% -> 0%
where the time goes in v1:
time: 124 us
  blocking collectives  73.3 us (59%)
  Pallas kernels  31.3 us (25%)
  waiting for transfers between devices  8.51 us (7%)
  local copies, waits for them, and re-layouts  4.14 us (3%)
  starting transfers between devices  3.5 us (3%)
  other arithmetic  1.52 us (1%)
    pallas_call x1, Pallas kernels, spatial(): pl.pallas_call(spatial_kernel, out_shape=jax.ShapeDtypeStruct((inp.shape[...  31.3 us
    all_to_all x1, blocking collectives, on_device(): lax.all_to_all(jnp.concatenate([masked, places], 1), CELL, 0, 0, tiled=True)  29.5 us
    all_to_all x1, blocking collectives, on_device(): lax.all_to_all(mixed_cells.reshape(cell_size * period_size, per_local, 12...  24.7 us
    all_to_all x1, blocking collectives, group_sum(): return jnp.sum(lax.all_to_all(spread, axes, 0, 0, tiled=True), axis=0)  10.7 us
    all_to_all x1, waiting for transfers between devices, group_sum(): return jnp.sum(lax.all_to_all(spread, axes, 0, 0, tiled=True), axis=0)  8.51 us
    all_to_all x1, blocking collectives, on_device(): lax.all_to_all(mixed.reshape(period_size, per_local, obs_count, 128), PER...  8.39 us
    all_to_all x1, starting transfers between devices, group_sum(): return jnp.sum(lax.all_to_all(spread, axes, 0, 0, tiled=True), axis=0)  3.5 us
  transfers between devices with their start and end apart: 1, of which 1 were waited for; matrix products, arithmetic and copies ran while one was open for 1% of the time, Pallas kernels for 0%

profile of v1, /device:TPU:1, one launch (start us, length us, event | category | flops | bytes accessed | tf_op | source)
XLA Modules:
  0.0 123.7 jit_solution(7869640282970174884)
XLA Ops:
  0.6 0.0 copy-start
  0.6 0.0 copy-start.1
  0.7 0.7 copy-done.1
  1.3 0.0 copy-start.2
  1.4 0.6 copy-done.2
  2.0 0.1 compare_convert_fusion
  2.1 0.1 copy.28
  2.2 1.1 broadcast_multiply_fusion
  3.3 0.1 broadcast_in_dim.8
  3.4 0.2 pad_maximum_fusion
  3.6 29.5 %all_to_all.27.inp_ref = f32[32,4,1024]{2,1,0:T(4,128)} all-to-all(f32[32,4,1024]{2,1,0:T(4,128)S(1)} %pad_maximum_fusion), channel_id=1, replica_groups=mesh['z'=8,'y_hi'=2,'core'=2,'x'=4,'y_lo'=2] {'z','y_hi','core'}, dimensions={0} | all-to-all | bytes 1048576 | tf_op jit(solution)/shard_map/all_to_all | solution.py:107
  33.1 31.3 %spatial.1 = f32[32,8,2,128]{3,2,1,0:T(2,128)} custom-call(f32[32,4,1024]{2,1,0:T(4,128)} %all_to_all.27.inp_ref, f32[256,512]{1,0:T(8,128)} %constant.20.clone.bxt_ref.bxi_ref, f32[256,512]{1,0:T(8,128)} %constant.20.clone.bxt_ref.bxi_ref, f32[256,128]{1,0:T(8,128)} %constant.21.clone.by_ref, f32[128,256]{1,0:T(8,128)} %constant.22.clone.byt_ref, ...), custom_call_target="tpu_custom_call" | custom-call | tf_op jit(solution)/shard_map/spatial/pallas_call | solution.py:81
  64.4 24.7 %all_to_all.28 = f32[256,2,128]{2,1,0:T(2,128)S(1)} all-to-all(f32[256,2,128]{2,1,0:T(2,128)} %bitcast.17), channel_id=1, replica_groups=mesh['z'=8,'y_hi'=2,'core'=2,'x'=4,'y_lo'=2] {'z','y_hi','core','x','y_lo'}, dimensions={0} | all-to-all | bytes 524288 | tf_op jit(solution)/shard_map/all_to_all | solution.py:109
  89.1 0.0 copy-done
  89.1 0.4 fusion.1
  89.5 0.1 copy.29
  89.6 8.4 %all_to_all.29 = f32[8,2,32,128]{3,1,2,0:T(2,128)S(1)} all-to-all(f32[8,2,32,128]{3,1,2,0:T(2,128)S(1)} %copy.29), channel_id=1, replica_groups=mesh['z'=8,'y_hi'=2,'core'=2,'x'=4,'y_lo'=2] {'x','y_lo'}, dimensions={0} | all-to-all | bytes 524288 | tf_op jit(solution)/shard_map/all_to_all | solution.py:114
  97.9 0.2 copy.30
  98.2 0.4 convolution_bitcast_fusion
  98.6 0.1 broadcast_in_dim.9
  98.7 10.7 %all_to_all.30 = f32[16,1,1024]{2,1,0:T(1,128)S(1)} all-to-all(f32[16,1,1024]{2,1,0:T(1,128)S(1)} %broadcast_in_dim.10), channel_id=1, replica_groups=mesh['z'=8,'y_hi'=2,'core'=2,'x'=4,'y_lo'=2] {'x','y_lo','core'}, dimensions={0} | all-to-all | bytes 131072 | tf_op jit(solution)/shard_map/all_to_all | solution.py:96
  109.3 0.1 reduce_sum.18
  109.4 0.7 broadcast_in_dim.11
  110.0 3.5 %all-to-all-start.4 = ((f32[16,1,1024]{2,1,0:T(1,128)}), f32[16,1,1024]{2,1,0:T(1,128)S(1)}, u32[]{:S(2)}, u32[]{:S(2)}) async-start(f32[16,1,1024]{2,1,0:T(1,128)} %broadcast_in_dim.11), calls=%async_computation.4 | async-start | bytes 131072 | tf_op jit(solution)/shard_map/all_to_all | solution.py:96
  113.5 0.9 copy.34
  114.4 8.5 %all-to-all-done.4 = f32[16,1,1024]{2,1,0:T(1,128)S(1)} async-done(((f32[16,1,1024]{2,1,0:T(1,128)}), f32[16,1,1024]{2,1,0:T(1,128)S(1)}, u32[]{:S(2)}, u32[]{:S(2)}) %all-to-all-start.4) | async-done | bytes 65568 | tf_op jit(solution)/shard_map/all_to_all | solution.py:96
  123.0 0.1 reduce_sum.19
  123.0 0.7 reshape.77
  (4 shorter events, 0.1 us)
Async XLA Ops:
  0.6 88.5 %copy-start = (f32[16,16]{1,0:T(8,128)S(1)}, f32[16,16]{1,0:T(8,128)}, u32[]{:S(2)}) copy-start(f32[16,16]{1,0:T(8,128)} %param.12) | copy-start | bytes 3076
  0.6 0.7 copy-start.1
  1.3 0.7 copy-start.2
  110.0 12.9 %all-to-all-start.4 = ((f32[16,1,1024]{2,1,0:T(1,128)}), f32[16,1,1024]{2,1,0:T(1,128)S(1)}, u32[]{:S(2)}, u32[]{:S(2)}) async-start(f32[16,1,1024]{2,1,0:T(1,128)} %broadcast_in_dim.11), calls=%async_computation.4 | async-start | bytes 131072 | tf_op jit(solution)/shard_map/all_to_all | solution.py:96

commit v2 on v0

v2 whole, which is shorter than its diff:
```python
import jax
import jax.numpy as jnp
import numpy as np
from jax import lax
from jax.experimental import pallas as pl
from jax.experimental.pallas import tpu as pltpu
from jax.sharding import Mesh, PartitionSpec as P

LENGTH_SCALE = 48.0
WIDTH, HEIGHT = 256, 128
BF16, F32 = jnp.bfloat16, jnp.float32
ROWS_BY_ROWS = (((1,), (1,)), ((), ()))


def real_basis(size, keep):
    wave = np.arange(size)
    freq = np.where(wave <= size // 2, wave, size - wave)
    angle = 2 * np.pi * ((freq[:, None] * np.arange(keep)[None, :]) % size) / size
    basis = np.where(wave[:, None] <= size // 2, np.cos(angle), np.sin(angle)) * np.sqrt(2.0 / size)
    basis[0] /= np.sqrt(2.0)
    basis[size // 2] /= np.sqrt(2.0)
    return basis, freq


def constants():
    basis_x, freq_x = real_basis(2 * WIDTH, WIDTH)
    basis_y, freq_y = real_basis(2 * HEIGHT, HEIGHT)
    gap_x = np.minimum(np.arange(2 * WIDTH), 2 * WIDTH - np.arange(2 * WIDTH))
    gap_y = np.minimum(np.arange(2 * HEIGHT), 2 * HEIGHT - np.arange(2 * HEIGHT))
    tile = np.exp(-np.sqrt(gap_y[:, None] ** 2.0 + gap_x[None, :] ** 2.0) / LENGTH_SCALE)
    spectrum = np.real(np.fft.fft2(tile))[freq_y][:, freq_x]
    return basis_x, basis_y, spectrum


def host_pieces(values, count):
    pieces, rest = [], np.asarray(values, np.float64)
    for _ in range(count):
        piece = rest.astype(np.float32).astype(BF16)
        pieces.append(piece)
        rest = rest - piece.astype(np.float64)
    return pieces


def pieces_of(values, count):
    pieces = []
    for _ in range(count):
        piece = values.astype(BF16)
        pieces.append(piece)
        values = values - piece.astype(F32)
    return pieces


def product(a, b):
    return jnp.dot(a, b, preferred_element_type=F32)


def spatial_kernel(rows_ref, fx_ref, fy_ref, iy_ref, ix_ref, lam_ref, out_ref, acc_ref, table_ref):
    lists, _, length = rows_ref.shape
    acc_ref[...] = jnp.zeros_like(acc_ref)

    def one_hot(index, count):
        ids = lax.broadcasted_iota(jnp.int32, (count, length), 0).astype(F32).astype(BF16)
        return ids == index.astype(BF16)

    def place(c, _):
        block = rows_ref[c]
        in_row = one_hot(block[3:4, :], HEIGHT)
        in_column = jnp.where(one_hot(block[2:3, :], WIDTH), BF16(1), BF16(0))
        pieces = [pieces_of(block[r : r + 1, :], 3) for r in range(2)]
        spread = [jnp.where(in_row, pieces[r][s], BF16(0)) for s in range(3) for r in range(2)]
        acc_ref[...] += lax.dot_general(
            jnp.concatenate(spread, 0), in_column, ROWS_BY_ROWS, preferred_element_type=F32
        )
        return 0

    lax.fori_loop(0, lists, place, 0, unroll=8)

    grid = acc_ref[...].astype(BF16)
    p0 = product(grid, fx_ref[0])
    p1 = product(grid[:512], fx_ref[1])
    p2 = product(grid[:256], fx_ref[2])
    along_x = p0[:256] + ((p0[256:512] + p1[:256]) + (p0[512:] + p1[256:] + p2))
    u = [jnp.concatenate([part[:128], part[128:]], 1) for part in pieces_of(along_x, 3)]
    waves = product(fy_ref[0], jnp.concatenate([u[0], u[1]], 0)) + (
        product(fy_ref[1], jnp.concatenate([u[0], u[1]], 0))
        + product(fy_ref[2], jnp.concatenate([u[0], u[2]], 0))
    )
    waves = waves * jnp.concatenate([lam_ref[...]] * 2, 1)
    w = pieces_of(waves, 2)
    q = product(iy_ref[...], w[0])
    v = q[:128] + (q[128:] + product(iy_ref[:128], w[1]))
    v = pieces_of(jnp.concatenate([v[:, :512], v[:, 512:]], 0), 2)
    q = lax.dot_general(ix_ref[...], v[0], ROWS_BY_ROWS, preferred_element_type=F32)
    field = q[:256] + (
        q[256:] + lax.dot_general(ix_ref[:256], v[1], ROWS_BY_ROWS, preferred_element_type=F32)
    )
    for s, part in enumerate(pieces_of(field, 2)):
        for r in range(2):
            for m in range(2):
                table_ref[256 * s + 128 * r : 256 * s + 128 * r + 128, 128 * m : 128 * m + 128] = part[
                    128 * m : 128 * m + 128, 128 * r : 128 * r + 128
                ]

    def pick(c, _):
        block = rows_ref[c]
        xs = block[2:3, :]
        half = jnp.where(xs >= 128.0, 128.0, 0.0)
        hot = jnp.where(one_hot(block[3:4, :] + half, 256), BF16(1), BF16(0))
        found = product(table_ref[...], hot)
        in_column = lax.broadcasted_iota(jnp.int32, (128, length), 0).astype(F32) == xs - half
        for r in range(2):
            both = found[128 * r : 128 * r + 128] + found[256 + 128 * r : 384 + 128 * r]
            value = jnp.sum(jnp.where(in_column, both, 0.0), 0, keepdims=True)
            for s in range(length // 128):
                out_ref[c, s, r : r + 1, :] = value[:, 128 * s : 128 * s + 128]
        return 0

    lax.fori_loop(0, lists, pick, 0, unroll=8)


def spatial(rows):
    basis_x, basis_y, spectrum = constants()
    x, y = host_pieces(basis_x, 3), host_pieces(basis_y, 3)
    forward_x = np.stack([part.T for part in x])
    forward_y = np.stack([np.concatenate(pair, 1) for pair in ((y[0], y[1]), (y[1], y[0]), (y[2], y[0]))])
    inverse_y = np.concatenate([y[0].T, y[1].T], 0)
    inverse_x = np.concatenate([x[0].T, x[1].T], 0)
    whole = pl.BlockSpec(memory_space=pltpu.VMEM)
    lists, _, length = rows.shape
    return pl.pallas_call(
        spatial_kernel,
        out_shape=jax.ShapeDtypeStruct((lists, length // 128, 2, 128), F32),
        in_specs=[whole] * 6,
        out_specs=whole,
        scratch_shapes=[pltpu.VMEM((768, 256), F32), pltpu.VMEM((512, 256), BF16)],
        compiler_params=pltpu.CompilerParams(vmem_limit_bytes=24 * 1024 * 1024),
        name="spatial",
    )(rows, jnp.asarray(forward_x), jnp.asarray(forward_y), jnp.asarray(inverse_y), jnp.asarray(inverse_x),
      jnp.asarray(spectrum, F32))


CELL = ("z", "y_hi", "core")
PERIOD = ("x", "y_lo")


def group_sum(values, axes, count):
    spread = jnp.broadcast_to(values[None], (count,) + values.shape)
    return jnp.sum(lax.all_to_all(spread, axes, 0, 0, tiled=True), axis=0)


def on_device(footprints, cell_coords, obs_period, temporal_cov):
    obs_count, per_local, cell_local = footprints.shape
    cell_size, period_size = 32, 8
    period_first = lax.axis_index(PERIOD) * per_local
    period_ids = period_first + jnp.arange(per_local, dtype=jnp.int32)
    keep = (period_ids[None, :, None] <= obs_period[:, None, None]).astype(jnp.float32)
    masked = footprints * keep
    places = jnp.broadcast_to(cell_coords.astype(jnp.float32)[None], (obs_count, 2, cell_local))
    rows = lax.all_to_all(jnp.concatenate([masked, places], 1), CELL, 0, 0, tiled=True)
    mixed_cells = spatial(rows)
    by_cell = lax.all_to_all(
        mixed_cells.reshape(cell_size * period_size, per_local, 128), CELL + PERIOD, 0, 0, tiled=True
    )
    by_cell = by_cell.reshape(obs_count, period_size * per_local, 128)
    mixed = jnp.einsum("tu,nuj->tnj", temporal_cov, by_cell, precision=lax.Precision.HIGHEST)
    mixed = lax.all_to_all(
        mixed.reshape(period_size, per_local, obs_count, 128), PERIOD, 0, 0, tiled=True
    )
    hq_field = jnp.transpose(mixed, (2, 1, 0, 3)).reshape(obs_count, per_local, cell_local)
    gram = jnp.einsum("ntj,mtj->nm", hq_field, masked, precision=lax.Precision.HIGHEST)
    gram = group_sum(gram.reshape(obs_count * obs_count), ("x", "y_lo", "core"), 16)
    gram = group_sum(gram, ("z", "y_hi"), 16)
    return (hq_field, gram.reshape(obs_count, obs_count))


def solution(mesh):
    fine = Mesh(mesh.devices.reshape(8, 2, 2, 4, 2), CELL + PERIOD)
    return jax.shard_map(
        on_device,
        mesh=fine,
        in_specs=(P(None, PERIOD, CELL), P(None, CELL), P(), P()),
        out_specs=(P(None, PERIOD, CELL), P()),
        check_vma=False,
    )
```

time: 413 us -> 118 us (0.29)
  matrix products: 160 us -> 0.75 us
  waiting for transfers between devices: 107 us -> 8.51 us
  blocking collectives: 125 us -> 73 us
  Pallas kernels: 0 us -> 25.2 us
  between operations: 14.1 us -> 0.8 us
    dot_general x9 -> x1, matrix products: 160 us -> 0.35 us  [on_device(): jnp.einsum('tu,nuj->tnj', temporal_cov, by_cell, precision=lax.Precision....]
    all_gather x2 -> x0, waiting for transfers between devices: 107 us -> none  [the longest x1 58.6 us: on_device(): piece_rows = lax.all_gather(flat_rows, 'cell', axis=1, tiled=True)]
    psum x1 -> x0, blocking collectives: 78.1 us -> none  [on_device(): hqh_gram = lax.psum(partial_gram, ('cell', 'period'))]
    all_to_all x0 -> x4, blocking collectives: none -> 73 us  [the longest x1 29.5 us: on_device(): lax.all_to_all(jnp.concatenate([masked, places], 1), CELL, 0, 0, tiled=True)]
    all_gather x1 -> x0, blocking collectives: 47.3 us -> none  [on_device(): piece_places = lax.all_gather(local_places, 'cell', axis=1, tiled=True)]
    pallas_call x0 -> x1, Pallas kernels: none -> 25.2 us  [spatial(): pl.pallas_call(spatial_kernel, out_shape=jax.ShapeDtypeStruct((lists, len...]
    all_to_all x0 -> x1, waiting for transfers between devices: none -> 8.51 us  [group_sum(): return jnp.sum(lax.all_to_all(spread, axes, 0, 0, tiled=True), axis=0)]
  transfers between devices with their start and end apart: 2 -> 1, of which waited for: 2 -> 1; matrix products, arithmetic and copies ran while one was open for 0% -> 1% of each run, Pallas kernels for 0% -> 0%
where the time goes in v2:
time: 118 us; the launch traced here: 117 us
  blocking collectives  73 us (62%)
  Pallas kernels  25.2 us (21%)
  waiting for transfers between devices  8.51 us (7%)
  local copies, waits for them, and re-layouts  4.18 us (4%)
  starting transfers between devices  3.49 us (3%)
  other arithmetic  1.52 us (1%)
    all_to_all x1, blocking collectives, on_device(): lax.all_to_all(jnp.concatenate([masked, places], 1), CELL, 0, 0, tiled=True)  29.5 us
    pallas_call x1, Pallas kernels, spatial(): pl.pallas_call(spatial_kernel, out_shape=jax.ShapeDtypeStruct((lists, len...  25.2 us
    all_to_all x1, blocking collectives, on_device(): lax.all_to_all(mixed_cells.reshape(cell_size * period_size, per_local, 12...  24.4 us
    all_to_all x1, blocking collectives, group_sum(): return jnp.sum(lax.all_to_all(spread, axes, 0, 0, tiled=True), axis=0)  10.7 us
    all_to_all x1, waiting for transfers between devices, group_sum(): return jnp.sum(lax.all_to_all(spread, axes, 0, 0, tiled=True), axis=0)  8.51 us
    all_to_all x1, blocking collectives, on_device(): lax.all_to_all(mixed.reshape(period_size, per_local, obs_count, 128), PER...  8.38 us
    all_to_all x1, starting transfers between devices, group_sum(): return jnp.sum(lax.all_to_all(spread, axes, 0, 0, tiled=True), axis=0)  3.49 us
  transfers between devices with their start and end apart: 1, of which 1 were waited for; matrix products, arithmetic and copies ran while one was open for 1% of the time, Pallas kernels for 0%

profile of v2, /device:TPU:1, one launch (start us, length us, event | category | flops | bytes accessed | tf_op | source)
XLA Modules:
  0.0 117.5 jit_solution(7517392875879258063)
XLA Ops:
  0.6 0.0 copy-start
  0.6 0.0 copy-start.6
  0.7 0.7 copy-done.6
  1.3 0.0 copy-start.7
  1.4 0.6 copy-done.7
  2.0 0.1 compare_convert_fusion
  2.1 0.1 copy.28
  2.2 1.1 broadcast_multiply_fusion
  3.3 0.0 copy-start.4
  3.3 0.1 broadcast_in_dim.8
  3.4 0.0 copy-start.2
  3.4 0.0 copy-start.3
  3.4 0.2 pad_maximum_fusion
  3.6 0.0 copy-start.1
  3.6 0.0 copy-start.5
  3.7 29.5 %all_to_all.27.rows_ref = f32[32,4,1024]{2,1,0:T(4,128)S(1)} all-to-all(f32[32,4,1024]{2,1,0:T(4,128)S(1)} %pad_maximum_fusion), channel_id=1, replica_groups=mesh['z'=8,'y_hi'=2,'core'=2,'x'=4,'y_lo'=2] {'z','y_hi','core'}, dimensions={0} | all-to-all | bytes 1048576 | tf_op jit(solution)/shard_map/all_to_all | solution.py:159
  33.2 0.0 copy-done.4
  33.2 0.0 copy-done.2
  33.2 0.0 copy-done.3
  33.2 0.0 copy-done.1
  33.2 0.0 copy-done.5
  33.2 25.2 %spatial.1 = f32[32,8,2,128]{3,2,1,0:T(2,128)S(1)} custom-call(f32[32,4,1024]{2,1,0:T(4,128)S(1)} %all_to_all.27.rows_ref, bf16[3,256,512]{2,1,0:T(8,128)(2,1)S(1)} %copy-done.1, bf16[3,256,256]{2,1,0:T(8,128)(2,1)S(1)} %copy-done.4, bf16[256,256]{1,0:T(8,128)(2,1)S(1)} %copy-done.5, bf16[512,512]{1,0:T(8,128)(2,1)S(1)} %copy-done.3, f32[256,512]{1,0:T(8,128)S(1)} %copy-done.2), custom_call_target="tpu_custom_call" | custom-call | tf_op jit(solution)/shard_map/spatial/pallas_call | solution.py:130
  58.4 24.4 %all_to_all.28 = f32[256,2,128]{2,1,0:T(2,128)S(1)} all-to-all(f32[256,2,128]{2,1,0:T(2,128)S(1)} %bitcast.17), channel_id=1, replica_groups=mesh['z'=8,'y_hi'=2,'core'=2,'x'=4,'y_lo'=2] {'z','y_hi','core','x','y_lo'}, dimensions={0} | all-to-all | bytes 524288 | tf_op jit(solution)/shard_map/all_to_all | solution.py:161
  82.9 0.0 copy-done
  82.9 0.3 fusion.1
  83.2 0.1 copy.29
  83.3 8.4 %all_to_all.29 = f32[8,2,32,128]{3,1,2,0:T(2,128)S(1)} all-to-all(f32[8,2,32,128]{3,1,2,0:T(2,128)S(1)} %copy.29), channel_id=1, replica_groups=mesh['z'=8,'y_hi'=2,'core'=2,'x'=4,'y_lo'=2] {'x','y_lo'}, dimensions={0} | all-to-all | bytes 524288 | tf_op jit(solution)/shard_map/all_to_all | solution.py:166
  91.7 0.2 copy.30
  91.9 0.4 convolution_bitcast_fusion
  92.3 0.1 broadcast_in_dim.9
  92.4 10.7 %all_to_all.30 = f32[16,1,1024]{2,1,0:T(1,128)S(1)} all-to-all(f32[16,1,1024]{2,1,0:T(1,128)S(1)} %broadcast_in_dim.10), channel_id=1, replica_groups=mesh['z'=8,'y_hi'=2,'core'=2,'x'=4,'y_lo'=2] {'x','y_lo','core'}, dimensions={0} | all-to-all | bytes 131072 | tf_op jit(solution)/shard_map/all_to_all | solution.py:148
  103.1 0.1 reduce_sum.18
  103.2 0.7 broadcast_in_dim.11
  103.8 3.5 %all-to-all-start.4 = ((f32[16,1,1024]{2,1,0:T(1,128)}), f32[16,1,1024]{2,1,0:T(1,128)S(1)}, u32[]{:S(2)}, u32[]{:S(2)}) async-start(f32[16,1,1024]{2,1,0:T(1,128)} %broadcast_in_dim.11), calls=%async_computation.4 | async-start | bytes 131072 | tf_op jit(solution)/shard_map/all_to_all | solution.py:148
  107.3 0.9 copy.34
  108.2 8.5 %all-to-all-done.4 = f32[16,1,1024]{2,1,0:T(1,128)S(1)} async-done(((f32[16,1,1024]{2,1,0:T(1,128)}), f32[16,1,1024]{2,1,0:T(1,128)S(1)}, u32[]{:S(2)}, u32[]{:S(2)}) %all-to-all-start.4) | async-done | bytes 65568 | tf_op jit(solution)/shard_map/all_to_all | solution.py:148
  116.7 0.1 reduce_sum.19
  116.8 0.7 reshape.77
  (4 shorter events, 0.1 us)
Async XLA Ops:
  0.6 82.2 %copy-start = (f32[16,16]{1,0:T(8,128)S(1)}, f32[16,16]{1,0:T(8,128)}, u32[]{:S(2)}) copy-start(f32[16,16]{1,0:T(8,128)} %param.12) | copy-start | bytes 3076
  0.6 0.7 copy-start.6
  1.3 0.7 copy-start.7
  3.3 29.9 %copy-start.4 = (bf16[3,256,256]{2,1,0:T(8,128)(2,1)S(1)}, bf16[3,256,256]{2,1,0:T(8,128)(2,1)}, u32[]{:S(2)}) copy-start(bf16[3,256,256]{2,1,0:T(8,128)(2,1)} %constant.23.clone.fy_ref) | copy-start | bytes 1179652
  3.4 29.8 %copy-start.2 = (f32[256,512]{1,0:T(8,128)S(1)}, f32[256,512]{1,0:T(8,128)}, u32[]{:S(2)}) copy-start(f32[256,512]{1,0:T(8,128)} %constant.26.clone.lam_ref) | copy-start | bytes 1572868
  3.4 29.8 %copy-start.3 = (bf16[512,512]{1,0:T(8,128)(2,1)S(1)}, bf16[512,512]{1,0:T(8,128)(2,1)}, u32[]{:S(2)}) copy-start(bf16[512,512]{1,0:T(8,128)(2,1)} %constant.25.clone.ix_ref) | copy-start | bytes 1572868
  3.6 29.6 %copy-start.1 = (bf16[3,256,512]{2,1,0:T(8,128)(2,1)S(1)}, bf16[3,256,512]{2,1,0:T(8,128)(2,1)}, u32[]{:S(2)}) copy-start(bf16[3,256,512]{2,1,0:T(8,128)(2,1)} %constant.22.clone.fx_ref) | copy-start | bytes 2359300
  3.6 29.6 %copy-start.5 = (bf16[256,256]{1,0:T(8,128)(2,1)S(1)}, bf16[256,256]{1,0:T(8,128)(2,1)}, u32[]{:S(2)}) copy-start(bf16[256,256]{1,0:T(8,128)(2,1)} %constant.24.clone.iy_ref) | copy-start | bytes 393220
  103.8 12.9 %all-to-all-start.4 = ((f32[16,1,1024]{2,1,0:T(1,128)}), f32[16,1,1024]{2,1,0:T(1,128)S(1)}, u32[]{:S(2)}, u32[]{:S(2)}) async-start(f32[16,1,1024]{2,1,0:T(1,128)} %broadcast_in_dim.11), calls=%async_computation.4 | async-start | bytes 131072 | tf_op jit(solution)/shard_map/all_to_all | solution.py:148

commit v3 on v2

--- a/solution.py
+++ b/solution.py
@@ -168,8 +168,8 @@
     )
     hq_field = jnp.transpose(mixed, (2, 1, 0, 3)).reshape(obs_count, per_local, cell_local)
     gram = jnp.einsum("ntj,mtj->nm", hq_field, masked, precision=lax.Precision.HIGHEST)
-    gram = group_sum(gram.reshape(obs_count * obs_count), ("x", "y_lo", "core"), 16)
-    gram = group_sum(gram, ("z", "y_hi"), 16)
+    gram = group_sum(gram.reshape(obs_count * obs_count), ("y_hi", "core", "x", "y_lo"), 32)
+    gram = group_sum(gram, ("z",), 8)
     return (hq_field, gram.reshape(obs_count, obs_count))
 
 

time: 118 us -> 117 us (level)
  waiting for transfers between devices: 8.51 us -> 5.89 us
  blocking collectives: 73 us -> 75.1 us
    all_to_all x1, waiting for transfers between devices: 8.51 us -> 5.89 us  [group_sum(): return jnp.sum(lax.all_to_all(spread, axes, 0, 0, tiled=True), axis=0)]
    all_to_all x1, blocking collectives: 10.7 us -> 12.7 us  [group_sum(): return jnp.sum(lax.all_to_all(spread, axes, 0, 0, tiled=True), axis=0)]
where the time goes in v3:
time: 117 us
  blocking collectives  75.1 us (64%)
  Pallas kernels  25.2 us (22%)
  waiting for transfers between devices  5.89 us (5%)
  local copies, waits for them, and re-layouts  4.18 us (4%)
  starting transfers between devices  3.33 us (3%)
  other arithmetic  1.54 us (1%)
    all_to_all x1, blocking collectives, on_device(): lax.all_to_all(jnp.concatenate([masked, places], 1), CELL, 0, 0, tiled=True)  29.5 us
    pallas_call x1, Pallas kernels, spatial(): pl.pallas_call(spatial_kernel, out_shape=jax.ShapeDtypeStruct((lists, len...  25.2 us
    all_to_all x1, blocking collectives, on_device(): lax.all_to_all(mixed_cells.reshape(cell_size * period_size, per_local, 12...  24.4 us
    all_to_all x1, blocking collectives, group_sum(): return jnp.sum(lax.all_to_all(spread, axes, 0, 0, tiled=True), axis=0)  12.7 us
    all_to_all x1, blocking collectives, on_device(): lax.all_to_all(mixed.reshape(period_size, per_local, obs_count, 128), PER...  8.38 us
    all_to_all x1, waiting for transfers between devices, group_sum(): return jnp.sum(lax.all_to_all(spread, axes, 0, 0, tiled=True), axis=0)  5.89 us
    all_to_all x1, starting transfers between devices, group_sum(): return jnp.sum(lax.all_to_all(spread, axes, 0, 0, tiled=True), axis=0)  3.33 us
  transfers between devices with their start and end apart: 1, of which 1 were waited for; matrix products, arithmetic and copies ran while one was open for 1% of the time, Pallas kernels for 0%

profile of v3, /device:TPU:1, one launch (start us, length us, event | category | flops | bytes accessed | tf_op | source)
XLA Modules:
  0.0 116.8 jit_solution(8551003920035994324)
XLA Ops:
  0.6 0.0 copy-start
  0.6 0.0 copy-start.6
  0.7 0.7 copy-done.6
  1.3 0.0 copy-start.7
  1.4 0.6 copy-done.7
  2.0 0.1 compare_convert_fusion
  2.1 0.1 copy.28
  2.2 1.1 broadcast_multiply_fusion
  3.3 0.0 copy-start.4
  3.3 0.1 broadcast_in_dim.8
  3.4 0.0 copy-start.2
  3.4 0.0 copy-start.3
  3.4 0.2 pad_maximum_fusion
  3.6 0.0 copy-start.1
  3.6 0.0 copy-start.5
  3.7 29.5 %all_to_all.27.rows_ref = f32[32,4,1024]{2,1,0:T(4,128)S(1)} all-to-all(f32[32,4,1024]{2,1,0:T(4,128)S(1)} %pad_maximum_fusion), channel_id=1, replica_groups=mesh['z'=8,'y_hi'=2,'core'=2,'x'=4,'y_lo'=2] {'z','y_hi','core'}, dimensions={0} | all-to-all | bytes 1048576 | tf_op jit(solution)/shard_map/all_to_all | solution.py:159
  33.2 0.0 copy-done.4
  33.2 0.0 copy-done.2
  33.2 0.0 copy-done.3
  33.2 0.0 copy-done.1
  33.2 0.0 copy-done.5
  33.2 25.2 %spatial.1 = f32[32,8,2,128]{3,2,1,0:T(2,128)S(1)} custom-call(f32[32,4,1024]{2,1,0:T(4,128)S(1)} %all_to_all.27.rows_ref, bf16[3,256,512]{2,1,0:T(8,128)(2,1)S(1)} %copy-done.1, bf16[3,256,256]{2,1,0:T(8,128)(2,1)S(1)} %copy-done.4, bf16[256,256]{1,0:T(8,128)(2,1)S(1)} %copy-done.5, bf16[512,512]{1,0:T(8,128)(2,1)S(1)} %copy-done.3, f32[256,512]{1,0:T(8,128)S(1)} %copy-done.2), custom_call_target="tpu_custom_call" | custom-call | tf_op jit(solution)/shard_map/spatial/pallas_call | solution.py:130
  58.4 24.4 %all_to_all.28 = f32[256,2,128]{2,1,0:T(2,128)S(1)} all-to-all(f32[256,2,128]{2,1,0:T(2,128)S(1)} %bitcast.17), channel_id=1, replica_groups=mesh['z'=8,'y_hi'=2,'core'=2,'x'=4,'y_lo'=2] {'z','y_hi','core','x','y_lo'}, dimensions={0} | all-to-all | bytes 524288 | tf_op jit(solution)/shard_map/all_to_all | solution.py:161
  82.9 0.0 copy-done
  82.9 0.3 fusion.1
  83.2 0.1 copy.29
  83.3 8.4 %all_to_all.29 = f32[8,2,32,128]{3,1,2,0:T(2,128)S(1)} all-to-all(f32[8,2,32,128]{3,1,2,0:T(2,128)S(1)} %copy.29), channel_id=1, replica_groups=mesh['z'=8,'y_hi'=2,'core'=2,'x'=4,'y_lo'=2] {'x','y_lo'}, dimensions={0} | all-to-all | bytes 524288 | tf_op jit(solution)/shard_map/all_to_all | solution.py:166
  91.7 0.2 copy.30
  91.9 0.4 convolution_bitcast_fusion
  92.3 0.1 broadcast_in_dim.9
  92.4 0.1 broadcast_in_dim.10
  92.5 12.7 %all_to_all.30 = f32[32,1,1024]{2,1,0:T(1,128)S(1)} all-to-all(f32[32,1,1024]{2,1,0:T(1,128)S(1)} %broadcast_in_dim.10), channel_id=1, replica_groups=mesh['z'=8,'y_hi'=2,'core'=2,'x'=4,'y_lo'=2] {'y_hi','core','x','y_lo'}, dimensions={0} | all-to-all | bytes 262144 | tf_op jit(solution)/shard_map/all_to_all | solution.py:148
  105.2 0.1 reduce_sum.18
  105.3 0.6 broadcast_in_dim.11
  105.9 3.3 %all-to-all-start.4 = ((f32[8,1,1024]{2,1,0:T(1,128)}), f32[8,1,1024]{2,1,0:T(1,128)S(1)}, u32[]{:S(2)}, u32[]{:S(2)}) async-start(f32[8,1,1024]{2,1,0:T(1,128)} %broadcast_in_dim.11), calls=%async_computation.4 | async-start | bytes 65536 | tf_op jit(solution)/shard_map/all_to_all | solution.py:148
  109.3 0.9 copy.34
  110.2 5.9 %all-to-all-done.4 = f32[8,1,1024]{2,1,0:T(1,128)S(1)} async-done(((f32[8,1,1024]{2,1,0:T(1,128)}), f32[8,1,1024]{2,1,0:T(1,128)S(1)}, u32[]{:S(2)}, u32[]{:S(2)}) %all-to-all-start.4) | async-done | bytes 32800 | tf_op jit(solution)/shard_map/all_to_all | solution.py:148
  116.1 0.7 reshape.77
  (4 shorter events, 0.1 us)
Async XLA Ops:
  0.6 82.2 %copy-start = (f32[16,16]{1,0:T(8,128)S(1)}, f32[16,16]{1,0:T(8,128)}, u32[]{:S(2)}) copy-start(f32[16,16]{1,0:T(8,128)} %param.12) | copy-start | bytes 3076
  0.6 0.7 copy-start.6
  1.3 0.7 copy-start.7
  3.3 29.9 %copy-start.4 = (bf16[3,256,256]{2,1,0:T(8,128)(2,1)S(1)}, bf16[3,256,256]{2,1,0:T(8,128)(2,1)}, u32[]{:S(2)}) copy-start(bf16[3,256,256]{2,1,0:T(8,128)(2,1)} %constant.23.clone.fy_ref) | copy-start | bytes 1179652
  3.4 29.8 %copy-start.2 = (f32[256,512]{1,0:T(8,128)S(1)}, f32[256,512]{1,0:T(8,128)}, u32[]{:S(2)}) copy-start(f32[256,512]{1,0:T(8,128)} %constant.26.clone.lam_ref) | copy-start | bytes 1572868
  3.4 29.8 %copy-start.3 = (bf16[512,512]{1,0:T(8,128)(2,1)S(1)}, bf16[512,512]{1,0:T(8,128)(2,1)}, u32[]{:S(2)}) copy-start(bf16[512,512]{1,0:T(8,128)(2,1)} %constant.25.clone.ix_ref) | copy-start | bytes 1572868
  3.6 29.6 %copy-start.1 = (bf16[3,256,512]{2,1,0:T(8,128)(2,1)S(1)}, bf16[3,256,512]{2,1,0:T(8,128)(2,1)}, u32[]{:S(2)}) copy-start(bf16[3,256,512]{2,1,0:T(8,128)(2,1)} %constant.22.clone.fx_ref) | copy-start | bytes 2359300
  3.6 29.6 %copy-start.5 = (bf16[256,256]{1,0:T(8,128)(2,1)S(1)}, bf16[256,256]{1,0:T(8,128)(2,1)}, u32[]{:S(2)}) copy-start(bf16[256,256]{1,0:T(8,128)(2,1)} %constant.24.clone.iy_ref) | copy-start | bytes 393220
  105.9 10.1 %all-to-all-start.4 = ((f32[8,1,1024]{2,1,0:T(1,128)}), f32[8,1,1024]{2,1,0:T(1,128)S(1)}, u32[]{:S(2)}, u32[]{:S(2)}) async-start(f32[8,1,1024]{2,1,0:T(1,128)} %broadcast_in_dim.11), calls=%async_computation.4 | async-start | bytes 65536 | tf_op jit(solution)/shard_map/all_to_all | solution.py:148

commit v4 on v3

--- a/solution.py
+++ b/solution.py
@@ -54,7 +54,7 @@
     return jnp.dot(a, b, preferred_element_type=F32)
 
 
-def spatial_kernel(rows_ref, fx_ref, fy_ref, iy_ref, ix_ref, lam_ref, out_ref, acc_ref, table_ref):
+def spatial_kernel(rows_ref, fx_ref, fy_ref, iy_ref, lam_ref, out_ref, acc_ref, table_ref):
     lists, _, length = rows_ref.shape
     acc_ref[...] = jnp.zeros_like(acc_ref)
 
@@ -73,7 +73,7 @@
         )
         return 0
 
-    lax.fori_loop(0, lists, place, 0, unroll=8)
+    lax.fori_loop(0, lists, place, 0, unroll=16)
 
     grid = acc_ref[...].astype(BF16)
     p0 = product(grid, fx_ref[0])
@@ -90,9 +90,10 @@
     q = product(iy_ref[...], w[0])
     v = q[:128] + (q[128:] + product(iy_ref[:128], w[1]))
     v = pieces_of(jnp.concatenate([v[:, :512], v[:, 512:]], 0), 2)
-    q = lax.dot_general(ix_ref[...], v[0], ROWS_BY_ROWS, preferred_element_type=F32)
+    inverse_x = fx_ref[:2].reshape(2 * WIDTH, 2 * WIDTH)
+    q = lax.dot_general(inverse_x, v[0], ROWS_BY_ROWS, preferred_element_type=F32)
     field = q[:256] + (
-        q[256:] + lax.dot_general(ix_ref[:256], v[1], ROWS_BY_ROWS, preferred_element_type=F32)
+        q[256:] + lax.dot_general(fx_ref[0], v[1], ROWS_BY_ROWS, preferred_element_type=F32)
     )
     for s, part in enumerate(pieces_of(field, 2)):
         for r in range(2):
@@ -115,7 +116,7 @@
                 out_ref[c, s, r : r + 1, :] = value[:, 128 * s : 128 * s + 128]
         return 0
 
-    lax.fori_loop(0, lists, pick, 0, unroll=8)
+    lax.fori_loop(0, lists, pick, 0, unroll=16)
 
 
 def spatial(rows):
@@ -124,18 +125,17 @@
     forward_x = np.stack([part.T for part in x])
     forward_y = np.stack([np.concatenate(pair, 1) for pair in ((y[0], y[1]), (y[1], y[0]), (y[2], y[0]))])
     inverse_y = np.concatenate([y[0].T, y[1].T], 0)
-    inverse_x = np.concatenate([x[0].T, x[1].T], 0)
     whole = pl.BlockSpec(memory_space=pltpu.VMEM)
     lists, _, length = rows.shape
     return pl.pallas_call(
         spatial_kernel,
         out_shape=jax.ShapeDtypeStruct((lists, length // 128, 2, 128), F32),
-        in_specs=[whole] * 6,
+        in_specs=[whole] * 5,
         out_specs=whole,
         scratch_shapes=[pltpu.VMEM((768, 256), F32), pltpu.VMEM((512, 256), BF16)],
         compiler_params=pltpu.CompilerParams(vmem_limit_bytes=24 * 1024 * 1024),
         name="spatial",
-    )(rows, jnp.asarray(forward_x), jnp.asarray(forward_y), jnp.asarray(inverse_y), jnp.asarray(inverse_x),
+    )(rows, jnp.asarray(forward_x), jnp.asarray(forward_y), jnp.asarray(inverse_y),
       jnp.asarray(spectrum, F32))
 
 

time: 117 us -> 116 us (level)
  no operation moved by 1% of the time
where the time goes in v4:
time: 116 us
  blocking collectives  75 us (65%)
  Pallas kernels  24.4 us (21%)
  waiting for transfers between devices  5.89 us (5%)
  local copies, waits for them, and re-layouts  4.17 us (4%)
  starting transfers between devices  3.33 us (3%)
  other arithmetic  1.54 us (1%)
    all_to_all x1, blocking collectives, on_device(): lax.all_to_all(jnp.concatenate([masked, places], 1), CELL, 0, 0, tiled=True)  29.5 us
    pallas_call x1, Pallas kernels, spatial(): pl.pallas_call(spatial_kernel, out_shape=jax.ShapeDtypeStruct((lists, len...  24.4 us
    all_to_all x1, blocking collectives, on_device(): lax.all_to_all(mixed_cells.reshape(cell_size * period_size, per_local, 12...  24.4 us
    all_to_all x1, blocking collectives, group_sum(): return jnp.sum(lax.all_to_all(spread, axes, 0, 0, tiled=True), axis=0)  12.7 us
    all_to_all x1, blocking collectives, on_device(): lax.all_to_all(mixed.reshape(period_size, per_local, obs_count, 128), PER...  8.38 us
    all_to_all x1, waiting for transfers between devices, group_sum(): return jnp.sum(lax.all_to_all(spread, axes, 0, 0, tiled=True), axis=0)  5.89 us
    all_to_all x1, starting transfers between devices, group_sum(): return jnp.sum(lax.all_to_all(spread, axes, 0, 0, tiled=True), axis=0)  3.33 us
  transfers between devices with their start and end apart: 1, of which 1 were waited for; matrix products, arithmetic and copies ran while one was open for 1% of the time, Pallas kernels for 0%

profile of v4, /device:TPU:1, one launch (start us, length us, event | category | flops | bytes accessed | tf_op | source)
XLA Modules:
  0.0 116.0 jit_solution(4161621081303265169)
XLA Ops:
  0.6 0.0 copy-start
  0.6 0.0 copy-start.5
  0.7 0.7 copy-done.5
  1.3 0.0 copy-start.6
  1.4 0.6 copy-done.6
  2.0 0.1 compare_convert_fusion
  2.1 0.1 copy.27
  2.2 1.1 broadcast_multiply_fusion
  3.3 0.1 broadcast_in_dim.8
  3.4 0.0 copy-start.1
  3.4 0.2 pad_maximum_fusion
  3.6 0.0 copy-start.2
  3.6 0.0 copy-start.3
  3.6 0.0 copy-start.4
  3.6 29.5 %all_to_all.27.rows_ref = f32[32,4,1024]{2,1,0:T(4,128)S(1)} all-to-all(f32[32,4,1024]{2,1,0:T(4,128)S(1)} %pad_maximum_fusion), channel_id=1, replica_groups=mesh['z'=8,'y_hi'=2,'core'=2,'x'=4,'y_lo'=2] {'z','y_hi','core'}, dimensions={0} | all-to-all | bytes 1048576 | tf_op jit(solution)/shard_map/all_to_all | solution.py:159
  33.2 0.0 copy-done.1
  33.2 0.0 copy-done.2
  33.2 0.0 copy-done.3
  33.2 0.0 copy-done.4
  33.2 24.4 %spatial.1 = f32[32,8,2,128]{3,2,1,0:T(2,128)S(1)} custom-call(f32[32,4,1024]{2,1,0:T(4,128)S(1)} %all_to_all.27.rows_ref, bf16[3,256,512]{2,1,0:T(8,128)(2,1)S(1)} %copy-done.1, bf16[3,256,256]{2,1,0:T(8,128)(2,1)S(1)} %copy-done.3, bf16[256,256]{1,0:T(8,128)(2,1)S(1)} %copy-done.4, f32[256,512]{1,0:T(8,128)S(1)} %copy-done.2), custom_call_target="tpu_custom_call" | custom-call | tf_op jit(solution)/shard_map/spatial/pallas_call | solution.py:130
  57.6 24.4 %all_to_all.28 = f32[256,2,128]{2,1,0:T(2,128)S(1)} all-to-all(f32[256,2,128]{2,1,0:T(2,128)S(1)} %bitcast.17), channel_id=1, replica_groups=mesh['z'=8,'y_hi'=2,'core'=2,'x'=4,'y_lo'=2] {'z','y_hi','core','x','y_lo'}, dimensions={0} | all-to-all | bytes 524288 | tf_op jit(solution)/shard_map/all_to_all | solution.py:161
  82.1 0.0 copy-done
  82.1 0.3 fusion.1
  82.4 0.1 copy.28
  82.5 8.4 %all_to_all.29 = f32[8,2,32,128]{3,1,2,0:T(2,128)S(1)} all-to-all(f32[8,2,32,128]{3,1,2,0:T(2,128)S(1)} %copy.28), channel_id=1, replica_groups=mesh['z'=8,'y_hi'=2,'core'=2,'x'=4,'y_lo'=2] {'x','y_lo'}, dimensions={0} | all-to-all | bytes 524288 | tf_op jit(solution)/shard_map/all_to_all | solution.py:166
  90.9 0.2 copy.29
  91.1 0.4 convolution_bitcast_fusion
  91.5 0.1 broadcast_in_dim.9
  91.6 0.1 broadcast_in_dim.10
  91.7 12.7 %all_to_all.30 = f32[32,1,1024]{2,1,0:T(1,128)S(1)} all-to-all(f32[32,1,1024]{2,1,0:T(1,128)S(1)} %broadcast_in_dim.10), channel_id=1, replica_groups=mesh['z'=8,'y_hi'=2,'core'=2,'x'=4,'y_lo'=2] {'y_hi','core','x','y_lo'}, dimensions={0} | all-to-all | bytes 262144 | tf_op jit(solution)/shard_map/all_to_all | solution.py:148
  104.4 0.1 reduce_sum.18
  104.5 0.6 broadcast_in_dim.11
  105.1 3.3 %all-to-all-start.4 = ((f32[8,1,1024]{2,1,0:T(1,128)}), f32[8,1,1024]{2,1,0:T(1,128)S(1)}, u32[]{:S(2)}, u32[]{:S(2)}) async-start(f32[8,1,1024]{2,1,0:T(1,128)} %broadcast_in_dim.11), calls=%async_computation.4 | async-start | bytes 65536 | tf_op jit(solution)/shard_map/all_to_all | solution.py:148
  108.4 0.9 copy.33
  109.3 5.9 %all-to-all-done.4 = f32[8,1,1024]{2,1,0:T(1,128)S(1)} async-done(((f32[8,1,1024]{2,1,0:T(1,128)}), f32[8,1,1024]{2,1,0:T(1,128)S(1)}, u32[]{:S(2)}, u32[]{:S(2)}) %all-to-all-start.4) | async-done | bytes 32800 | tf_op jit(solution)/shard_map/all_to_all | solution.py:148
  115.3 0.7 reshape.77
  (4 shorter events, 0.1 us)
Async XLA Ops:
  0.6 81.4 %copy-start = (f32[16,16]{1,0:T(8,128)S(1)}, f32[16,16]{1,0:T(8,128)}, u32[]{:S(2)}) copy-start(f32[16,16]{1,0:T(8,128)} %param.11) | copy-start | bytes 3076
  0.6 0.7 copy-start.5
  1.3 0.7 copy-start.6
  3.4 29.8 %copy-start.1 = (bf16[3,256,512]{2,1,0:T(8,128)(2,1)S(1)}, bf16[3,256,512]{2,1,0:T(8,128)(2,1)}, u32[]{:S(2)}) copy-start(bf16[3,256,512]{2,1,0:T(8,128)(2,1)} %constant.20.clone.fx_ref) | copy-start | bytes 2359300
  3.6 29.6 %copy-start.2 = (f32[256,512]{1,0:T(8,128)S(1)}, f32[256,512]{1,0:T(8,128)}, u32[]{:S(2)}) copy-start(f32[256,512]{1,0:T(8,128)} %constant.23.clone.lam_ref) | copy-start | bytes 1572868
  3.6 29.6 %copy-start.3 = (bf16[3,256,256]{2,1,0:T(8,128)(2,1)S(1)}, bf16[3,256,256]{2,1,0:T(8,128)(2,1)}, u32[]{:S(2)}) copy-start(bf16[3,256,256]{2,1,0:T(8,128)(2,1)} %constant.21.clone.fy_ref) | copy-start | bytes 1179652
  3.6 29.6 %copy-start.4 = (bf16[256,256]{1,0:T(8,128)(2,1)S(1)}, bf16[256,256]{1,0:T(8,128)(2,1)}, u32[]{:S(2)}) copy-start(bf16[256,256]{1,0:T(8,128)(2,1)} %constant.22.clone.iy_ref) | copy-start | bytes 393220
  105.1 10.1 %all-to-all-start.4 = ((f32[8,1,1024]{2,1,0:T(1,128)}), f32[8,1,1024]{2,1,0:T(1,128)S(1)}, u32[]{:S(2)}, u32[]{:S(2)}) async-start(f32[8,1,1024]{2,1,0:T(1,128)} %broadcast_in_dim.11), calls=%async_computation.4 | async-start | bytes 65536 | tf_op jit(solution)/shard_map/all_to_all | solution.py:148
